TPU v7x, 256 devices: a whole 4x4x8 slice. The times are simulated.
256 devices in a mesh: row: 16 (over y_hi, x, core), col: 16 (over z, y_lo).
Axes of the slice: x: 4, y: 4 (y_hi: 2, y_lo: 2; y = y_hi * 2 + y_lo), z: 8, core: 2. Of those that a mesh axis runs over, the one named last changes fastest.
Arguments:
- factor_a: bfloat16 [128, 32768], P('row', 'col'), may hold values from -12 to 12
- factor_b: bfloat16 [128, 32768], P('row', 'col'), may hold values from -12 to 12
- pair: bfloat16 [1024, 1024, 128], P('row', 'col'), may hold values from -6 to 6
- proj_weight: bfloat16 [1024, 128], replicated, may hold values from -0.1875 to 0.1875
- proj_bias: float32 [128], replicated, may hold values from -3 to 3
- norm_gain: float32 [128], replicated, may hold values from 0.25 to 1.75
- norm_bias: float32 [128], replicated, may hold values from -3 to 3
- trans_in: bfloat16 [128, 1024], replicated, may hold values from -0.5 to 0.5
- trans_out: bfloat16 [512, 128], replicated, may hold values from -0.25 to 0.25
- cotangent: bfloat16 [1024, 1024, 128], P('row', 'col'), may hold values from -6 to 6
Outputs:
- new_pair: bfloat16 [1024, 1024, 128], P('row', 'col')
- pair_grad: bfloat16 [1024, 1024, 128], P('row', 'col')
- grad_a: float32 [128, 32768], P('row', 'col')
- grad_b: float32 [128, 32768], P('row', 'col')
All inputs are finite; a program needn't handle non-finite values.
Results may differ from a plain program's by a relative error of at most 0.006.
Values may be sent and summed in bfloat16 or wider, within the bound.
A program may use at most 64 MiB of HBM per device.

v0:
```python
import jax
import jax.numpy as jnp
from jax import lax
from jax.sharding import PartitionSpec as P

H = 32


def copy_for_each(array, axis):
    copies = jnp.broadcast_to(array, (lax.axis_size(axis), *array.shape))
    return lax.all_to_all(copies, axis, split_axis=0, concat_axis=0, tiled=True)


def joined_along(tiles, dim):
    tiles = jnp.moveaxis(tiles, 0, dim)
    lengths = tiles.shape
    return tiles.reshape(*lengths[:dim], lengths[dim] * lengths[dim + 1], *lengths[dim + 2 :])


def gather_directly(array, axis, dim):
    tiles = copy_for_each(array, axis)
    return joined_along(tiles, dim)


def in_blocks(array, dim, peers):
    before, after = (array.shape[:dim], array.shape[dim + 1 :])
    return jnp.moveaxis(array.reshape(*before, peers, -1, *after), dim, 0)


def sum_at_owner(array, axis, dim):
    peers = lax.axis_size(axis)
    tiles = lax.all_to_all(in_blocks(array, dim, peers), axis, 0, 0, tiled=True)
    return jnp.sum(tiles, axis=0)


def dot_last(left, right):
    return lax.dot_general(
        left, right, (((1,), (1,)), ((), ())), preferred_element_type=jnp.float32
    )


def dot_first(left, right):
    return lax.dot_general(
        left, right, (((0,), (0,)), ((), ())), preferred_element_type=jnp.float32
    )


def factor_pull(grad_rows, proj_weight, seq_count, hidden_dim):
    rows_i, cols_j, width = grad_rows.shape
    weight_cube = proj_weight.reshape(hidden_dim, hidden_dim, width)
    pulled = (
        jnp.einsum("abc,hkc->ahbk", grad_rows, weight_cube, preferred_element_type=jnp.float32)
        / seq_count
    )
    pulled = pulled.astype(jnp.bfloat16)
    return pulled.reshape(rows_i * hidden_dim, cols_j * hidden_dim)


def pair_update(
    a_block,
    b_cols,
    pair_rows,
    cot_rows,
    proj_weight,
    proj_bias,
    norm_gain,
    norm_bias,
    trans_in,
    trans_out,
    seq_count,
    hidden_dim,
):
    rows_i, cols_j, width = pair_rows.shape
    units = trans_out.shape[0]
    outer = (dot_first(a_block, b_cols) / seq_count).astype(jnp.bfloat16)
    outer = outer.reshape(rows_i, hidden_dim, cols_j, hidden_dim)
    weight_cube = proj_weight.reshape(hidden_dim, hidden_dim, width)
    projected = jnp.einsum("ahbk,hkc->abc", outer, weight_cube, preferred_element_type=jnp.float32)
    updated = pair_rows.reshape(rows_i * cols_j, width).astype(jnp.float32)
    updated = updated + projected.reshape(rows_i * cols_j, width) + proj_bias
    row_mean = jnp.mean(updated, axis=-1, keepdims=True)
    centered = updated - row_mean
    row_var = jnp.mean(centered * centered, axis=-1, keepdims=True)
    inv_std = lax.rsqrt(row_var + 1e-05)
    normed = centered * inv_std
    lnorm = (normed * norm_gain + norm_bias).astype(jnp.bfloat16)
    both_pre = jnp.dot(lnorm, trans_in, preferred_element_type=jnp.float32)
    gate_pre = both_pre[:, :units]
    up_pre = both_pre[:, units:]
    sig_gate = jax.nn.sigmoid(gate_pre)
    activated = gate_pre * sig_gate
    hidden = (activated * up_pre).astype(jnp.bfloat16)
    new_rows = (updated + jnp.dot(hidden, trans_out, preferred_element_type=jnp.float32)).astype(
        jnp.bfloat16
    )
    cot_flat = cot_rows.reshape(rows_i * cols_j, width)
    d_hidden = dot_last(cot_flat, trans_out)
    d_gate = d_hidden * up_pre * sig_gate * (1.0 + gate_pre * (1.0 - sig_gate))
    d_up = d_hidden * activated
    d_both = jnp.concatenate([d_gate, d_up], axis=-1).astype(jnp.bfloat16)
    d_norm = dot_last(d_both, trans_in) * norm_gain
    d_mean = jnp.mean(d_norm, axis=-1, keepdims=True)
    d_proj = jnp.mean(d_norm * normed, axis=-1, keepdims=True)
    grad_flat = cot_flat.astype(jnp.float32) + inv_std * (d_norm - d_mean - normed * d_proj)
    grad_rows = grad_flat.astype(jnp.bfloat16).reshape(rows_i, cols_j, width)
    pulled = factor_pull(grad_rows, proj_weight, seq_count, hidden_dim)
    return (new_rows.reshape(rows_i, cols_j, width), grad_rows, pulled)


def pick_rows(rows_here, cols_here):
    target = max(8, 1024 // cols_here)
    block_rows = 8
    for candidate in range(8, rows_here + 1, 8):
        if rows_here % candidate == 0 and candidate <= target:
            block_rows = candidate
    return block_rows


def body(
    factor_a,
    factor_b,
    pair,
    proj_weight,
    proj_bias,
    norm_gain,
    norm_bias,
    trans_in,
    trans_out,
    cotangent,
):
    rows_here, cols_here, width = pair.shape
    seq_count = factor_a.shape[0] * lax.axis_size("row")
    block_rows = pick_rows(rows_here, cols_here)
    blocks = rows_here // block_rows
    gathered = gather_directly(factor_a, "col", 1)
    own_rows = lax.all_to_all(gathered, "row", split_axis=1, concat_axis=0, tiled=True)
    b_cols = lax.all_gather(factor_b, "row", axis=0, tiled=True)
    a_blocks = own_rows.reshape(seq_count, blocks, block_rows * H).transpose(1, 0, 2)
    pair_blocks = pair.reshape(blocks, block_rows, cols_here, width)
    cot_blocks = cotangent.reshape(blocks, block_rows, cols_here, width)

    def one_block(inputs_now):
        a_block, pair_rows, cot_rows = inputs_now
        new_rows, grad_rows, pulled = pair_update(
            a_block,
            b_cols,
            pair_rows,
            cot_rows,
            proj_weight,
            proj_bias,
            norm_gain,
            norm_bias,
            trans_in,
            trans_out,
            seq_count,
            H,
        )
        grad_a_block = dot_last(b_cols, pulled)
        return (new_rows, grad_rows, grad_a_block, pulled, a_block)

    def advance_sum(running, inputs_now):
        new_rows, grad_rows, grad_a_block, pulled, a_block = one_block(inputs_now)
        running = running + jnp.dot(a_block, pulled, preferred_element_type=jnp.float32)
        return (running, (new_rows, grad_rows, grad_a_block))

    start_sum = jnp.zeros((seq_count, cols_here * H), jnp.float32)
    column_sum, outputs = lax.scan(advance_sum, start_sum, (a_blocks, pair_blocks, cot_blocks))
    new_stack, grad_stack, part_stack = outputs
    grad_b = sum_at_owner(column_sum, "row", 0)
    new_pair = new_stack.reshape(rows_here, cols_here, width)
    pair_grad = grad_stack.reshape(rows_here, cols_here, width)
    grad_a_part = part_stack.transpose(1, 0, 2).reshape(seq_count, rows_here * H)
    returned = lax.all_to_all(grad_a_part, "row", split_axis=0, concat_axis=1, tiled=True)
    grad_a = sum_at_owner(returned, "col", 1)
    return (new_pair, pair_grad, grad_a, grad_b)


def solution(mesh):
    placed = (
        P("row", "col"),
        P("row", "col"),
        P("row", "col", None),
        P(),
        P(),
        P(),
        P(),
        P(),
        P(),
        P("row", "col", None),
    )
    return jax.shard_map(
        body,
        mesh=mesh,
        in_specs=placed,
        out_specs=(P("row", "col", None), P("row", "col", None), P("row", "col"), P("row", "col")),
        check_vma=False,
    )
```

profile of v0, /device:TPU:65, one launch (start us, length us, event | category | flops | bytes accessed | tf_op | source)
XLA Modules:
  0.0 376.8 jit_solution(9204570722906093368)
XLA Ops:
  1.5 24.0 %all_to_all.41 = bf16[16,8,2048]{2,1,0:T(8,128)(2,1)} all-to-all(bf16[16,8,2048]{2,1,0:T(8,128)(2,1)S(1)} %broadcast_in_dim.30), channel_id=1, replica_groups=mesh['row'=16,'col'=16] {'col'}, dimensions={0} | all-to-all | bytes 1048576 | tf_op jit(solution)/shard_map/all_to_all | solution.py:11
  25.5 7.7 %all-to-all-start.1 = ((bf16[8,16,2048]{2,0,1:T(8,128)(2,1)}), bf16[8,16,2048]{2,0,1:T(8,128)(2,1)S(1)}, u32[]{:S(2)}, u32[]{:S(2)}) async-start(bf16[8,16,2048]{2,0,1:T(8,128)(2,1)} %bitcast), calls=%async_computation.1 | async-start | bytes 1048576 | tf_op jit(solution)/shard_map/all_to_all | solution.py:136
  33.3 26.0 %all_gather.3 = bf16[128,2048]{1,0:T(8,128)(2,1)S(1)} all-gather(bf16[8,2048]{1,0:T(8,128)(2,1)S(1)} %copy-done.3), channel_id=1, replica_groups=mesh['row'=16,'col'=16] {'row'}, dimensions={0}, use_global_device_ids=true | all-gather | bytes 557056 | tf_op jit(solution)/shard_map/all_gather | solution.py:137
  60.6 240.0 %while.17 = (s32[]{:T(128)}, f32[128,2048]{1,0:T(8,128)}, bf16[4,16,64,128]{3,2,1,0:T(8,128)(2,1)}, bf16[4,16,64,128]{3,2,1,0:T(8,128)(2,1)}, f32[4,128,512]{1,2...) while((s32[]{:T(128)}, f32[128,2048]{1,0:T(8,128)}, ...), condition=%wide.region_5.6_spmd.clone, body=%wide.region_0.5_spmd.clone.sunk | while | flops 2170160128 | bytes 61169836 | solution.py:167
  62.3 8.0 %reshape.106 = bf16[16,32,64,32]{3,2,1,0:T(8,128)(2,1)} reshape(bf16[512,2048]{1,0:T(8,128)(2,1)S(1)} %multiply_convert_fusion.10) | data formatting | bytes 4194304 | tf_op jit(solution)/shard_map/while/body/eval_jaxpr/reshape | solution.py:76
  70.3 8.9 %copy.25 = bf16[16,64,32,32]{1,0,3,2:T(8,128)(2,1)} copy(bf16[16,64,32,32]{3,1,2,0:T(8,128)(2,1)} %bitcast.114) | data formatting | bytes 4194304 | tf_op jit(solution)/shard_map/while/body/eval_jaxpr/ahbk,hkc->abc/dot_general | solution.py:78
  79.2 5.5 %dot_general.46 = bf16[1024,32,32]{0,2,1:T(8,128)(2,1)S(1)} reshape(bf16[16,64,32,32]{1,0,3,2:T(8,128)(2,1)} %copy.25) | data formatting | bytes 4194304 | tf_op jit(solution)/shard_map/while/body/eval_jaxpr/ahbk,hkc->abc/dot_general | solution.py:78
  93.7 3.2 fusion.81
  97.0 8.4 %copy.26 = bf16[16,32,64,32]{3,2,1,0:T(8,128)(2,1)} copy(bf16[16,32,64,32]{2,3,1,0:T(8,128)(2,1)} %fusion.81) | data formatting | bytes 4194304 | tf_op jit(solution)/shard_map/while/body/eval_jaxpr/convert_element_type | solution.py:55
  105.4 11.1 %reshape.107 = bf16[512,2048]{1,0:T(8,128)(2,1)S(1)} reshape(bf16[16,32,64,32]{3,2,1,0:T(8,128)(2,1)} %copy.26) | data formatting | bytes 4194304 | tf_op jit(solution)/shard_map/while/body/eval_jaxpr/reshape | solution.py:56
  122.0 8.0 %reshape.106 = bf16[16,32,64,32]{3,2,1,0:T(8,128)(2,1)} reshape(bf16[512,2048]{1,0:T(8,128)(2,1)S(1)} %multiply_convert_fusion.10) | data formatting | bytes 4194304 | tf_op jit(solution)/shard_map/while/body/eval_jaxpr/reshape | solution.py:76
  130.0 8.9 %copy.25 = bf16[16,64,32,32]{1,0,3,2:T(8,128)(2,1)} copy(bf16[16,64,32,32]{3,1,2,0:T(8,128)(2,1)} %bitcast.114) | data formatting | bytes 4194304 | tf_op jit(solution)/shard_map/while/body/eval_jaxpr/ahbk,hkc->abc/dot_general | solution.py:78
  138.9 5.5 %dot_general.46 = bf16[1024,32,32]{0,2,1:T(8,128)(2,1)S(1)} reshape(bf16[16,64,32,32]{1,0,3,2:T(8,128)(2,1)} %copy.25) | data formatting | bytes 4194304 | tf_op jit(solution)/shard_map/while/body/eval_jaxpr/ahbk,hkc->abc/dot_general | solution.py:78
  153.4 3.2 fusion.81
  156.7 8.4 %copy.26 = bf16[16,32,64,32]{3,2,1,0:T(8,128)(2,1)} copy(bf16[16,32,64,32]{2,3,1,0:T(8,128)(2,1)} %fusion.81) | data formatting | bytes 4194304 | tf_op jit(solution)/shard_map/while/body/eval_jaxpr/convert_element_type | solution.py:55
  165.1 11.1 %reshape.107 = bf16[512,2048]{1,0:T(8,128)(2,1)S(1)} reshape(bf16[16,32,64,32]{3,2,1,0:T(8,128)(2,1)} %copy.26) | data formatting | bytes 4194304 | tf_op jit(solution)/shard_map/while/body/eval_jaxpr/reshape | solution.py:56
  182.1 8.0 %reshape.106 = bf16[16,32,64,32]{3,2,1,0:T(8,128)(2,1)} reshape(bf16[512,2048]{1,0:T(8,128)(2,1)S(1)} %multiply_convert_fusion.10) | data formatting | bytes 4194304 | tf_op jit(solution)/shard_map/while/body/eval_jaxpr/reshape | solution.py:76
  190.1 8.9 %copy.25 = bf16[16,64,32,32]{1,0,3,2:T(8,128)(2,1)} copy(bf16[16,64,32,32]{3,1,2,0:T(8,128)(2,1)} %bitcast.114) | data formatting | bytes 4194304 | tf_op jit(solution)/shard_map/while/body/eval_jaxpr/ahbk,hkc->abc/dot_general | solution.py:78
  199.0 5.5 %dot_general.46 = bf16[1024,32,32]{0,2,1:T(8,128)(2,1)S(1)} reshape(bf16[16,64,32,32]{1,0,3,2:T(8,128)(2,1)} %copy.25) | data formatting | bytes 4194304 | tf_op jit(solution)/shard_map/while/body/eval_jaxpr/ahbk,hkc->abc/dot_general | solution.py:78
  213.5 3.2 fusion.81
  216.8 8.4 %copy.26 = bf16[16,32,64,32]{3,2,1,0:T(8,128)(2,1)} copy(bf16[16,32,64,32]{2,3,1,0:T(8,128)(2,1)} %fusion.81) | data formatting | bytes 4194304 | tf_op jit(solution)/shard_map/while/body/eval_jaxpr/convert_element_type | solution.py:55
  225.2 11.1 %reshape.107 = bf16[512,2048]{1,0:T(8,128)(2,1)S(1)} reshape(bf16[16,32,64,32]{3,2,1,0:T(8,128)(2,1)} %copy.26) | data formatting | bytes 4194304 | tf_op jit(solution)/shard_map/while/body/eval_jaxpr/reshape | solution.py:56
  242.2 8.0 %reshape.106 = bf16[16,32,64,32]{3,2,1,0:T(8,128)(2,1)} reshape(bf16[512,2048]{1,0:T(8,128)(2,1)S(1)} %multiply_convert_fusion.10) | data formatting | bytes 4194304 | tf_op jit(solution)/shard_map/while/body/eval_jaxpr/reshape | solution.py:76
  250.2 8.9 %copy.25 = bf16[16,64,32,32]{1,0,3,2:T(8,128)(2,1)} copy(bf16[16,64,32,32]{3,1,2,0:T(8,128)(2,1)} %bitcast.114) | data formatting | bytes 4194304 | tf_op jit(solution)/shard_map/while/body/eval_jaxpr/ahbk,hkc->abc/dot_general | solution.py:78
  259.1 5.5 %dot_general.46 = bf16[1024,32,32]{0,2,1:T(8,128)(2,1)S(1)} reshape(bf16[16,64,32,32]{1,0,3,2:T(8,128)(2,1)} %copy.25) | data formatting | bytes 4194304 | tf_op jit(solution)/shard_map/while/body/eval_jaxpr/ahbk,hkc->abc/dot_general | solution.py:78
  273.6 3.2 fusion.81
  276.9 8.4 %copy.26 = bf16[16,32,64,32]{3,2,1,0:T(8,128)(2,1)} copy(bf16[16,32,64,32]{2,3,1,0:T(8,128)(2,1)} %fusion.81) | data formatting | bytes 4194304 | tf_op jit(solution)/shard_map/while/body/eval_jaxpr/convert_element_type | solution.py:55
  285.3 11.1 %reshape.107 = bf16[512,2048]{1,0:T(8,128)(2,1)S(1)} reshape(bf16[16,32,64,32]{3,2,1,0:T(8,128)(2,1)} %copy.26) | data formatting | bytes 4194304 | tf_op jit(solution)/shard_map/while/body/eval_jaxpr/reshape | solution.py:56
  303.1 21.1 %all_to_all.42 = f32[16,8,2048]{2,1,0:T(8,128)} all-to-all(f32[16,8,2048]{2,1,0:T(8,128)S(1)} %all_to_all.32), channel_id=1, replica_groups=mesh['row'=16,'col'=16] {'row'}, dimensions={0} | all-to-all | bytes 2097152 | tf_op jit(solution)/shard_map/all_to_all | solution.py:173
  324.2 20.6 %all_to_all.43 = f32[16,8,2048]{2,1,0:T(8,128)S(1)} all-to-all(f32[16,8,2048]{2,1,0:T(8,128)S(1)} %bitcast.117), channel_id=1, replica_groups=mesh['row'=16,'col'=16] {'row'}, dimensions={0} | all-to-all | bytes 2097152 | tf_op jit(solution)/shard_map/all_to_all | solution.py:32
  344.8 5.2 %all-to-all-start.3 = ((f32[16,8,2048]{2,1,0:T(8,128)}), f32[16,8,2048]{2,1,0:T(8,128)S(1)}, u32[]{:S(2)}, u32[]{:S(2)}) async-start(f32[16,8,2048]{2,1,0:T(8,128)} %all_to_all.42), calls=%async_computation.3 | async-start | bytes 2097152 | tf_op jit(solution)/shard_map/all_to_all | solution.py:32
  350.7 25.5 %all-to-all-done.3 = f32[16,8,2048]{2,1,0:T(8,128)S(1)} async-done(((f32[16,8,2048]{2,1,0:T(8,128)}), f32[16,8,2048]{2,1,0:T(8,128)S(1)}, u32[]{:S(2)}, u32[]{:S(2)}) %all-to-all-start.3) | async-done | bytes 1048608 | tf_op jit(solution)/shard_map/all_to_all | solution.py:32
  (96 shorter events, 64.8 us)
Async XLA Ops:
  0.6 32.7 %copy-start.3 = (bf16[8,2048]{1,0:T(8,128)(2,1)S(1)}, bf16[8,2048]{1,0:T(8,128)(2,1)}, u32[]{:S(2)}) copy-start(bf16[8,2048]{1,0:T(8,128)(2,1)} %param.13) | copy-start | bytes 98308
  25.5 35.1 %copy-start.1 = (bf16[1024,128]{1,0:T(8,128)(2,1)S(1)}, bf16[1024,128]{1,0:T(8,128)(2,1)}, u32[]{:S(2)}) copy-start(bf16[1024,128]{1,0:T(8,128)(2,1)} %param.15) | copy-start | bytes 786436
  25.5 35.1 %copy-start.2 = (bf16[128,1024]{1,0:T(8,128)(2,1)S(1)}, bf16[128,1024]{1,0:T(8,128)(2,1)}, u32[]{:S(2)}) copy-start(bf16[128,1024]{1,0:T(8,128)(2,1)} %param.19) | copy-start | bytes 786436
  25.5 35.1 %copy-start.4 = (f32[128]{0:T(128)S(1)}, f32[128]{0:T(128)}, u32[]{:S(2)}) copy-start(f32[128]{0:T(128)} %param.17) | copy-start | bytes 1540
  25.5 35.1 %copy-start.5 = (f32[128]{0:T(128)S(1)}, f32[128]{0:T(128)}, u32[]{:S(2)}) copy-start(f32[128]{0:T(128)} %param.18) | copy-start | bytes 1540
  25.5 35.1 %copy-start.6 = (bf16[512,128]{1,0:T(8,128)(2,1)S(1)}, bf16[512,128]{1,0:T(8,128)(2,1)}, u32[]{:S(2)}) copy-start(bf16[512,128]{1,0:T(8,128)(2,1)} %param.20) | copy-start | bytes 393220
  25.5 35.1 %copy-start.7 = (f32[128]{0:T(128)S(1)}, f32[128]{0:T(128)}, u32[]{:S(2)}) copy-start(f32[128]{0:T(128)} %param.16) | copy-start | bytes 1540
  25.5 33.8 %all-to-all-start.1 = ((bf16[8,16,2048]{2,0,1:T(8,128)(2,1)}), bf16[8,16,2048]{2,0,1:T(8,128)(2,1)S(1)}, u32[]{:S(2)}, u32[]{:S(2)}) async-start(bf16[8,16,2048]{2,0,1:T(8,128)(2,1)} %bitcast), calls=%async_computation.1 | async-start | bytes 1048576 | tf_op jit(solution)/shard_map/all_to_all | solution.py:136
  302.4 21.8 %copy-start = (f32[128,2048]{1,0:T(8,128)S(1)}, f32[128,2048]{1,0:T(8,128)}, u32[]{:S(2)}) copy-start(f32[128,2048]{1,0:T(8,128)} %get-tuple-element.87) | copy-start | bytes 3145732
  344.8 31.3 %all-to-all-start.3 = ((f32[16,8,2048]{2,1,0:T(8,128)}), f32[16,8,2048]{2,1,0:T(8,128)S(1)}, u32[]{:S(2)}, u32[]{:S(2)}) async-start(f32[16,8,2048]{2,1,0:T(8,128)} %all_to_all.42), calls=%async_computation.3 | async-start | bytes 2097152 | tf_op jit(solution)/shard_map/all_to_all | solution.py:32
where the time goes:
time: 383 us; the launch traced here: 377 us
  local copies, waits for them, and re-layouts  184 us (48%)
  blocking collectives  91.7 us (24%)
  matrix products  56.7 us (15%)
  waiting for transfers between devices  25.5 us (7%)
  starting transfers between devices  12.9 us (3%)
  other arithmetic  5.4 us (1%)
    dot_general x8, local copies, waits for them, and re-layouts, pair_update(): jnp.einsum('ahbk,hkc->abc', outer, weight_cube, preferred_element_type=jn...  57.5 us
    reshape x4, local copies, waits for them, and re-layouts, factor_pull(): return pulled.reshape(rows_i * hidden_dim, cols_j * hidden_dim)  44.4 us
    convert_element_type x4, local copies, waits for them, and re-layouts, factor_pull(): pulled = pulled.astype(jnp.bfloat16)  33.7 us
    reshape x4, local copies, waits for them, and re-layouts, pair_update(): outer = outer.reshape(rows_i, hidden_dim, cols_j, hidden_dim)  32.2 us
    all_gather x1, blocking collectives, body(): b_cols = lax.all_gather(factor_b, 'row', axis=0, tiled=True)  26 us
    all_to_all x1, waiting for transfers between devices, sum_at_owner(): tiles = lax.all_to_all(in_blocks(array, dim, peers), axis, 0, 0, tiled=True)  25.5 us
    all_to_all x1, blocking collectives, copy_for_each(): return lax.all_to_all(copies, axis, split_axis=0, concat_axis=0, tiled=True)  24 us
    all_to_all x1, blocking collectives, body(): lax.all_to_all(grad_a_part, 'row', split_axis=0, concat_axis=1, tiled=True)  21.1 us
  transfers between devices with their start and end apart: 2, of which 1 were waited for; matrix products, arithmetic and copies ran while one was open for 0% of the time, Pallas kernels for 0%

commit v1 on v0

v1 whole, which is shorter than its diff:
```python
import functools
import jax
import jax.numpy as jnp
from jax import lax
from jax.experimental import pallas as pl
from jax.experimental.pallas import tpu as pltpu
from jax.sharding import PartitionSpec as P

F32, BF16 = jnp.float32, jnp.bfloat16


def dot(x, y):
    return jnp.dot(x, y, preferred_element_type=F32)


def turned(x):
    return x.astype(F32).T.astype(BF16)


def prepare_weights(proj_weight, trans_in, trans_out, wide, w_bd, w_bdt, wi, wit, wot):
    wide[0:1024, :] = proj_weight[...].astype(F32) * (1.0 / 128)
    w_bd[...] = jnp.zeros(w_bd.shape, BF16)
    for q in range(16):
        for p in range(2):
            piece = wide[pl.ds(p * 16 + q, 32, stride=32), :].astype(BF16)
            for k in range(2):
                w_bd[q * 128 + p * 64 + k * 32 : q * 128 + p * 64 + k * 32 + 32, k * 128 : k * 128 + 128] = piece
    for q in range(16):
        w_bdt[:, q * 128 : q * 128 + 128] = turned(w_bd[q * 128 : q * 128 + 128, :])
    wi[:, 0:512] = (trans_in[:, 0:512].astype(F32) * 0.5).astype(BF16)
    wi[:, 512:1024] = trans_in[:, 512:1024]
    for q in range(8):
        wit[q * 128 : q * 128 + 128, :] = turned(wi[:, q * 128 : q * 128 + 128])
    for q in range(4):
        wot[:, q * 128 : q * 128 + 128] = turned(trans_out[q * 128 : q * 128 + 128, :])


def prepare_b(b_parts, wide, b_l, b_lt):
    for q in range(16):
        chunk = b_parts[:, :, q * 128 : q * 128 + 128].astype(F32).reshape(128, 128)
        wide[q * 128 : q * 128 + 128, :] = chunk.T
    for q in range(16):
        for p in range(2):
            piece = wide[pl.ds(p * 16 + q, 64, stride=32), :]
            b_l[q * 64 : q * 64 + 64, p * 128 : p * 128 + 128] = piece.astype(BF16)
    for q in range(8):
        b_lt[:, q * 128 : q * 128 + 128] = turned(b_l[q * 128 : q * 128 + 128, :])


def prepare_a(a_parts, a_bd, a_bdt, q):
    chunk = a_parts[:, :, q * 128 : q * 128 + 128].astype(F32).reshape(128, 128)
    other = pltpu.roll(chunk, 64, 1)
    low = lax.broadcasted_iota(jnp.int32, (128, 128), 1) < 64
    zero = jnp.zeros((128, 128), F32)
    at = q * 256
    a_bd[0:128, at : at + 128] = jnp.where(low, chunk, zero).astype(BF16)
    a_bd[128:256, at : at + 128] = jnp.where(low, zero, other).astype(BF16)
    a_bd[0:128, at + 128 : at + 256] = jnp.where(low, other, zero).astype(BF16)
    a_bd[128:256, at + 128 : at + 256] = jnp.where(low, zero, chunk).astype(BF16)
    across = chunk.T.astype(BF16)
    half = jnp.zeros((64, 128), BF16)
    for k in range(2):
        rows = across[k * 64 : k * 64 + 64, :]
        a_bdt[at + k * 128 : at + k * 128 + 64, 0:128] = rows
        a_bdt[at + k * 128 : at + k * 128 + 64, 128:256] = half
        a_bdt[at + k * 128 + 64 : at + k * 128 + 128, 0:128] = half
        a_bdt[at + k * 128 + 64 : at + k * 128 + 128, 128:256] = rows


def fold(y, n):
    out = []
    low = lax.broadcasted_iota(jnp.int32, (128, 128), 1) < 64
    for m in range(0, n, 2):
        e0 = y[0:128, m * 128 : m * 128 + 128]
        e1 = y[128:256, m * 128 : m * 128 + 128]
        o0 = y[0:128, m * 128 + 128 : m * 128 + 256]
        o1 = y[128:256, m * 128 + 128 : m * 128 + 256]
        out.append(jnp.where(low, e0, o1) + pltpu.roll(jnp.where(low, o0, e1), 64, 1))
    return out


def pair_block(ib, nb, pair, cot, bias, gain, shift, wi, wit, wo, wot, b_l, b_lt, a_bd, a_bdt, w_bd, w_bdt, xs, ps, new_pair, pair_grad):
    at = pl.multiple_of(ib * (nb * 128), nb * 128)
    rows = nb * 128
    for t in range(nb // 2):
        x = dot(b_l[...], a_bd[:, pl.ds(at + t * 256, 256)]).astype(BF16)
        for q in range(16):
            for k in range(2):
                xs[(2 * t + k) * 64 : (2 * t + k) * 64 + 64, q * 128 : q * 128 + 128] = x[q * 64 : q * 64 + 64, k * 128 : k * 128 + 128]
    proj = dot(xs[...], w_bd[...])
    proj = jnp.concatenate([proj[(k // 2) * 64 : (k // 2) * 64 + 64, (k % 2) * 128 : (k % 2) * 128 + 128] for k in range(2 * nb)], axis=0)
    first = pl.multiple_of(ib * rows, rows)
    updated = pair[pl.ds(first, rows), :].astype(F32) + (proj + bias[...])
    mu = jnp.mean(updated, axis=-1, keepdims=True)
    centered = updated - mu
    var = jnp.mean(centered * centered, axis=-1, keepdims=True)
    inv = lax.rsqrt(var + 1e-05)
    normed = centered * inv
    ln = (normed * gain[...] + shift[...]).astype(BF16)
    cot_here = cot[pl.ds(first, rows), :]
    both = dot(ln, wi[...])
    dh = dot(cot_here, wot[...])
    half = both[:, 0:512]
    up = both[:, 512:1024]
    q = 1.0 + jnp.tanh(half)
    act = half * q
    hidden = (act * up).astype(BF16)
    new_pair[pl.ds(first, rows), :] = (updated + dot(hidden, wo[...])).astype(BF16)
    d_up = (dh * act).astype(BF16)
    d_gate = (dh * up * (q + act * (2.0 - q))).astype(BF16)
    dn = (dot(d_gate, wit[0:512, :]) + dot(d_up, wit[512:1024, :])) * gain[...]
    m1 = jnp.mean(dn, axis=-1, keepdims=True)
    m2 = jnp.mean(dn * normed, axis=-1, keepdims=True)
    g = (cot_here.astype(F32) + inv * (dn - m1 - normed * m2)).astype(BF16)
    pair_grad[pl.ds(first, rows), :] = g
    g2 = jnp.concatenate(
        [jnp.concatenate([g[(2 * k) * 64 : (2 * k) * 64 + 64], g[(2 * k + 1) * 64 : (2 * k + 1) * 64 + 64]], axis=1) for k in range(nb)], axis=0
    )
    for t in range(8):
        pulled = dot(g2, w_bdt[:, t * 256 : t * 256 + 256]).astype(BF16)
        for k in range(nb):
            for m in range(2):
                q = 2 * t + m
                ps[q * 64 : q * 64 + 64, k * 128 : k * 128 + 128] = pulled[k * 64 : k * 64 + 64, m * 128 : m * 128 + 128]


MESH = pl.DeviceIdType.MESH
NB = 16
PEERS = 16


def here():
    return lax.axis_index("row"), lax.axis_index("col")


def greet(devices, count):
    barrier = pltpu.get_barrier_semaphore()
    for ok, where in devices:
        if ok is None:
            pl.semaphore_signal(barrier, inc=1, device_id=where, device_id_type=MESH)
        else:

            @pl.when(ok)
            def _(where=where):
                pl.semaphore_signal(barrier, inc=1, device_id=where, device_id_type=MESH)

    pl.semaphore_wait(barrier, count)


def gather_kernel(a, b, a_parts, b_parts, a_send, a_recv, b_send, b_recv):
    r, c = here()
    diagonal = r == c
    greetings = [(None, ((r + k) % PEERS, c)) for k in range(1, PEERS)]
    greetings += [(((r + k) % PEERS != r) | (c != r), ((r + k) % PEERS, r)) for k in range(PEERS)]
    greet(greetings, 2 * PEERS - 1 - diagonal.astype(jnp.int32))

    def b_copy(k):
        return pltpu.make_async_remote_copy(
            src_ref=b, dst_ref=b_parts.at[r], send_sem=b_send.at[k], recv_sem=b_recv.at[r],
            device_id=((r + k) % PEERS, c), device_id_type=MESH)

    def a_copy(k):
        return pltpu.make_async_remote_copy(
            src_ref=a, dst_ref=a_parts.at[r], send_sem=a_send.at[k], recv_sem=a_recv.at[r],
            device_id=(c, (c + k) % PEERS), device_id_type=MESH)

    own_b = pltpu.make_async_copy(b, b_parts.at[r], b_recv.at[r])
    own_b.start()
    own_a = pltpu.make_async_copy(a, a_parts.at[r], a_recv.at[r])

    @pl.when(diagonal)
    def _():
        own_a.start()

    @pl.when(jnp.logical_not(diagonal))
    def _():
        a_copy(0).start()

    for k in range(1, PEERS):
        a_copy(k).start()
        b_copy(k).start()

    for k in range(PEERS):
        pltpu.make_async_copy(b, b_parts.at[k], b_recv.at[k]).wait()
        pltpu.make_async_copy(a, a_parts.at[k], a_recv.at[k]).wait()
    for k in range(1, PEERS):
        a_copy(k).wait_send()
        b_copy(k).wait_send()

    @pl.when(jnp.logical_not(diagonal))
    def _():
        a_copy(0).wait_send()


def gather(a, b):
    vm = pl.BlockSpec(memory_space=pltpu.VMEM)
    return pl.pallas_call(
        gather_kernel,
        out_shape=(jax.ShapeDtypeStruct((PEERS, *a.shape), BF16),) * 2,
        in_specs=[vm] * 2,
        out_specs=(vm,) * 2,
        scratch_shapes=[pltpu.SemaphoreType.DMA((PEERS,))] * 4,
        compiler_params=pltpu.CompilerParams(collective_id=0, has_side_effects=True),
        name="gather",
    )(a, b)


def scatter_kernel(ga, gb, grad_a, grad_b, a_in, b_in, wide, a_send, a_recv, b_send, b_recv):
    r, c = here()
    diagonal = r == c
    greetings = [(None, ((r + k) % PEERS, c)) for k in range(1, PEERS)]
    greetings += [(((c + k) % PEERS != c) | (c != r), (c, (c + k) % PEERS)) for k in range(PEERS)]
    greet(greetings, 2 * PEERS - 1 - diagonal.astype(jnp.int32))

    def a_copy(k):
        to = (r + k) % PEERS
        return pltpu.make_async_remote_copy(
            src_ref=ga.at[to], dst_ref=a_in.at[c], send_sem=a_send.at[k], recv_sem=a_recv.at[c],
            device_id=(to, r), device_id_type=MESH)

    def b_copy(k):
        to = (r + k) % PEERS
        return pltpu.make_async_remote_copy(
            src_ref=gb.at[to], dst_ref=b_in.at[r], send_sem=b_send.at[k], recv_sem=b_recv.at[r],
            device_id=(to, c), device_id_type=MESH)

    pltpu.make_async_copy(gb.at[r], b_in.at[r], b_recv.at[r]).start()

    @pl.when(diagonal)
    def _():
        pltpu.make_async_copy(ga.at[r], a_in.at[c], a_recv.at[c]).start()

    @pl.when(jnp.logical_not(diagonal))
    def _():
        a_copy(0).start()

    for k in range(1, PEERS):
        a_copy(k).start()
        b_copy(k).start()

    for k in range(PEERS):
        pltpu.make_async_copy(gb.at[k], b_in.at[k], b_recv.at[k]).wait()
        pltpu.make_async_copy(ga.at[k], a_in.at[k], a_recv.at[k]).wait()
    for k in range(1, PEERS):
        a_copy(k).wait_send()
        b_copy(k).wait_send()

    @pl.when(jnp.logical_not(diagonal))
    def _():
        a_copy(0).wait_send()

    finish_a(a_in, grad_a)
    finish_b(b_in, wide, grad_b)


def finish_a(a_in, grad_a):
    for t in range(8):
        total = jnp.sum(a_in[:, :, t * 128 : t * 128 + 128].astype(F32), axis=0)
        blk, sub = t // 4, t % 4
        for k in range(2):
            at = blk * 1024 + k * 512 + sub * 128
            grad_a[:, at : at + 128] = total[k * 8 : k * 8 + 8]


def finish_b(b_in, wide, grad_b):
    for t in range(8):
        total = jnp.sum(b_in[:, :, t * 128 : t * 128 + 128].astype(F32), axis=0)
        across = jnp.concatenate([total, jnp.zeros((112, 128), F32)], axis=0).T
        for k in range(2):
            q = 2 * t + k
            rows = across[k * 64 : k * 64 + 64]
            wide[pl.ds(q, 64, stride=32), :] = rows
            wide[pl.ds(16 + q, 64, stride=32), :] = pltpu.roll(rows, 120, 1)
    for t in range(16):
        grad_b[:, t * 128 : t * 128 + 128] = wide[t * 128 : t * 128 + 128, :].T[0:8]


def scatter(ga, gb):
    vm = pl.BlockSpec(memory_space=pltpu.VMEM)
    return pl.pallas_call(
        scatter_kernel,
        out_shape=(jax.ShapeDtypeStruct((8, 2048), F32),) * 2,
        in_specs=[vm] * 2,
        out_specs=(vm,) * 2,
        scratch_shapes=[
            pltpu.VMEM((PEERS, 16, 1024), BF16),
            pltpu.VMEM((PEERS, 16, 1024), BF16),
            pltpu.VMEM((2048, 128), F32),
        ]
        + [pltpu.SemaphoreType.DMA((PEERS,))] * 4,
        compiler_params=pltpu.CompilerParams(collective_id=1, has_side_effects=True),
        name="scatter",
    )(ga, gb)


def tile_kernel(nb, a_parts, b_parts, pair, cot, proj_weight, bias, gain, shift, trans_in, trans_out, new_pair, pair_grad, ga, gb,
                wide, w_bd, w_bdt, wi, wit, wot, b_l, b_lt, a_bd, a_bdt, xs, ps, acc):
    prepare_weights(proj_weight, trans_in, trans_out, wide, w_bd, w_bdt, wi, wit, wot)
    prepare_b(b_parts, wide, b_l, b_lt)
    for q in range(16):
        prepare_a(a_parts, a_bd, a_bdt, q)
    acc[...] = jnp.zeros(acc.shape, F32)

    def step(ib, _):
        pair_block(ib, nb, pair, cot, bias, gain, shift, wi, wit, trans_out, wot, b_l, b_lt, a_bd, a_bdt, w_bd, w_bdt, xs, ps, new_pair, pair_grad)
        pieces = fold(dot(b_lt[...], ps[...]), nb)
        at = pl.multiple_of(ib * (nb * 32), nb * 32)
        for m in range(nb // 4):
            two = [pieces[m + k * (nb // 4)].reshape(PEERS, 8, 128) for k in range(2)]
            ga[:, :, pl.ds(at + m * 128, 128)] = jnp.concatenate(two, axis=1).astype(BF16)
        start = pl.multiple_of(ib * (nb * 128), nb * 128)
        acc[...] += dot(ps[...], a_bdt[pl.ds(start, nb * 128), :])
        return 0

    lax.fori_loop(0, 32 // nb, step, 0)
    for q in range(8):
        across = acc[q * 128 : q * 128 + 128, :].T
        two = [across[p * 128 : p * 128 + 128].reshape(PEERS, 8, 128) for p in range(2)]
        gb[:, :, q * 128 : q * 128 + 128] = jnp.concatenate(two, axis=1).astype(BF16)


def tile_call(nb, a_parts, b_parts, pair, cot, proj_weight, bias, gain, shift, trans_in, trans_out):
    S = jax.ShapeDtypeStruct
    vm = pl.BlockSpec(memory_space=pltpu.VMEM)
    return pl.pallas_call(
        functools.partial(tile_kernel, nb),
        out_shape=(S((4096, 128), BF16), S((4096, 128), BF16), S((16, 16, 1024), BF16), S((16, 16, 1024), BF16)),
        in_specs=[vm] * 10,
        out_specs=(vm,) * 4,
        scratch_shapes=[
            pltpu.VMEM((2048, 128), F32),
            pltpu.VMEM((2048, 256), BF16),
            pltpu.VMEM((256, 2048), BF16),
            pltpu.VMEM((128, 1024), BF16),
            pltpu.VMEM((1024, 128), BF16),
            pltpu.VMEM((128, 512), BF16),
            pltpu.VMEM((1024, 256), BF16),
            pltpu.VMEM((256, 1024), BF16),
            pltpu.VMEM((256, 4096), BF16),
            pltpu.VMEM((4096, 256), BF16),
            pltpu.VMEM((nb * 64, 2048), BF16),
            pltpu.VMEM((1024, nb * 128), BF16),
            pltpu.VMEM((1024, 256), F32),
        ],
        compiler_params=pltpu.CompilerParams(vmem_limit_bytes=58 << 20),
        name="tile",
    )(a_parts, b_parts, pair, cot, proj_weight, bias, gain, shift, trans_in, trans_out)


def body(factor_a, factor_b, pair, proj_weight, proj_bias, norm_gain, norm_bias, trans_in, trans_out, cotangent):
    a_parts, b_parts = gather(factor_a, factor_b)
    new_pair, pair_grad, ga, gb = tile_call(
        NB, a_parts, b_parts, pair.reshape(4096, 128), cotangent.reshape(4096, 128), proj_weight,
        proj_bias.reshape(1, 128), norm_gain.reshape(1, 128), norm_bias.reshape(1, 128), trans_in, trans_out)
    grad_a, grad_b = scatter(ga, gb)
    return new_pair.reshape(pair.shape), pair_grad.reshape(pair.shape), grad_a, grad_b


def solution(mesh):
    tiles = P("row", "col", None)
    return jax.shard_map(
        body,
        mesh=mesh,
        in_specs=(P("row", "col"), P("row", "col"), tiles, P(), P(), P(), P(), P(), P(), tiles),
        out_specs=(tiles, tiles, P("row", "col"), P("row", "col")),
        check_vma=False,
    )
```

time: 383 us -> 125 us (0.33); the launches traced: 377 us -> 125 us
  local copies, waits for them, and re-layouts: 184 us -> 2.14 us
  Pallas kernels: 0 us -> 122 us
  blocking collectives: 91.7 us -> 0 us
  matrix products: 56.7 us -> 0 us
  waiting for transfers between devices: 25.5 us -> 0 us
  starting transfers between devices: 12.9 us -> 0 us
  other arithmetic: 5.4 us -> 0 us
    pallas_call x0 -> x3, Pallas kernels: none -> 122 us  [the longest x1 61.2 us: scatter(): pl.pallas_call(scatter_kernel, out_shape=(jax.ShapeDtypeStruct((8, 2048),...]
    reshape x9 -> x0, local copies, waits for them, and re-layouts: 77 us -> none  [the longest x4 44.4 us: factor_pull(): return pulled.reshape(rows_i * hidden_dim, cols_j * hidden_dim)]
    all_to_all x3 -> x0, blocking collectives: 65.7 us -> none  [the longest x1 24 us: copy_for_each(): return lax.all_to_all(copies, axis, split_axis=0, concat_axis=0, tiled=True)]
    dot_general x8 -> x0, local copies, waits for them, and re-layouts: 57.5 us -> none  [pair_update(): jnp.einsum('ahbk,hkc->abc', outer, weight_cube, preferred_element_type=jn...]
    dot_general x36 -> x0, matrix products: 56.7 us -> none  [the longest x12 15.8 us: dot_last(): lax.dot_general(left, right, (((1,), (1,)), ((), ())), preferred_element_...]
    convert_element_type x4 -> x0, local copies, waits for them, and re-layouts: 33.7 us -> none  [factor_pull(): pulled = pulled.astype(jnp.bfloat16)]
    all_gather x1 -> x0, blocking collectives: 26 us -> none  [body(): b_cols = lax.all_gather(factor_b, 'row', axis=0, tiled=True)]
    all_to_all x2 -> x0, waiting for transfers between devices: 25.5 us -> none  [the longest x1 25.5 us: sum_at_owner(): tiles = lax.all_to_all(in_blocks(array, dim, peers), axis, 0, 0, tiled=True)]
  transfers between devices with their start and end apart: 2 -> 0, of which waited for: 1 -> 0; matrix products, arithmetic and copies ran while one was open for 0% -> 0% of each run, Pallas kernels for 0% -> 0%
where the time goes in v1:
time: 125 us
  Pallas kernels  122 us (98%)
  local copies, waits for them, and re-layouts  2.14 us (2%)
    pallas_call x1, Pallas kernels, scatter(): pl.pallas_call(scatter_kernel, out_shape=(jax.ShapeDtypeStruct((8, 2048),...  61.2 us
    pallas_call x1, Pallas kernels, tile_call(): pl.pallas_call(functools.partial(tile_kernel, nb), out_shape=(S((4096, 12...  33.2 us
    pallas_call x1, Pallas kernels, gather(): pl.pallas_call(gather_kernel, out_shape=(jax.ShapeDtypeStruct((PEERS, *a....  27.7 us

profile of v1, /device:TPU:65, one launch (start us, length us, event | category | flops | bytes accessed | tf_op | source)
XLA Modules:
  0.0 124.9 jit_solution(10822246113804913275)
XLA Ops:
  0.6 27.7 %gather.1 = (bf16[16,8,2048]{2,1,0:T(8,128)(2,1)}, bf16[16,8,2048]{2,1,0:T(8,128)(2,1)}) custom-call(bf16[8,2048]{1,0:T(8,128)(2,1)} %a.1, bf16[8,2048]{1,0:T(8,128)(2,1)} %b.1), custom_call_target="tpu_custom_call" | custom-call | tf_op jit(solution)/shard_map/gather/pallas_call | solution.py:197
  28.3 33.2 %tile.1 = (bf16[4096,128]{1,0:T(8,128)(2,1)}, bf16[4096,128]{1,0:T(8,128)(2,1)}, bf16[16,16,1024]{2,1,0:T(8,128)(2,1)}, bf16[16,16,1024]{2,1,0:T(8,128)(2,1)}) custom-call(bf16[16,8,2048]{2,1,0:T(8,128)(2,1)} %get-tuple-element.12.a_parts, bf16[16,8,2048]{2,1,0:T(8,128)(2,1)} %get-tuple-element.13.b_parts, bf16[4096,128]{1,0:T(8,128)(2,1)} %bitcast.7, ...), custom_call_target="tpu_custom_call" | custom-call | tf_op jit(solution)/shard_map/tile/pallas_call | solution.py:325
  61.5 61.2 %scatter.1 = (f32[8,2048]{1,0:T(8,128)}, f32[8,2048]{1,0:T(8,128)}) custom-call(bf16[16,16,1024]{2,1,0:T(8,128)(2,1)} %get-tuple-element.16.ga, bf16[16,16,1024]{2,1,0:T(8,128)(2,1)} %get-tuple-element.17.gb), custom_call_target="tpu_custom_call" | custom-call | tf_op jit(solution)/shard_map/scatter/pallas_call | solution.py:280
  122.7 0.0 copy-start
  122.7 1.5 %copy.16 = f32[8,2048]{1,0:T(8,128)} copy(f32[8,2048]{1,0:T(8,128)} %get-tuple-element.26) | data formatting | bytes 131072
  124.2 0.0 copy-done
  124.2 0.6 copy.17
Async XLA Ops:
  122.7 1.5 %copy-start = (f32[8,2048]{1,0:T(8,128)S(1)}, f32[8,2048]{1,0:T(8,128)}, u32[]{:S(2)}) copy-start(f32[8,2048]{1,0:T(8,128)} %get-tuple-element.27) | copy-start | bytes 196612

commit v2 on v1

v2 whole, which is shorter than its diff:
```python
import functools
import jax
import jax.numpy as jnp
from jax import lax
from jax.experimental import pallas as pl
from jax.experimental.pallas import tpu as pltpu
from jax.sharding import PartitionSpec as P

F32, BF16 = jnp.float32, jnp.bfloat16


def dot(x, y):
    return jnp.dot(x, y, preferred_element_type=F32)


def turned(x):
    return x.astype(F32).T.astype(BF16)


def prepare_weights(proj_weight, trans_in, trans_out, wide, w_bd, w_bdt, wi, wit, wot):
    wide[0:1024, :] = proj_weight[...].astype(F32) * (1.0 / 128)
    w_bd[...] = jnp.zeros(w_bd.shape, BF16)
    for q in range(16):
        for p in range(2):
            piece = wide[pl.ds(p * 16 + q, 32, stride=32), :].astype(BF16)
            for k in range(2):
                w_bd[q * 128 + p * 64 + k * 32 : q * 128 + p * 64 + k * 32 + 32, k * 128 : k * 128 + 128] = piece
    for q in range(16):
        w_bdt[:, q * 128 : q * 128 + 128] = turned(w_bd[q * 128 : q * 128 + 128, :])
    wi[:, 0:512] = (trans_in[:, 0:512].astype(F32) * 0.5).astype(BF16)
    wi[:, 512:1024] = trans_in[:, 512:1024]
    for q in range(8):
        wit[q * 128 : q * 128 + 128, :] = turned(wi[:, q * 128 : q * 128 + 128])
    for q in range(4):
        wot[:, q * 128 : q * 128 + 128] = turned(trans_out[q * 128 : q * 128 + 128, :])


def prepare_b(b_parts, wide, b_l, b_lt):
    for q in range(16):
        chunk = b_parts[:, :, q * 128 : q * 128 + 128].astype(F32).reshape(128, 128)
        wide[q * 128 : q * 128 + 128, :] = chunk.T
    for q in range(16):
        for p in range(2):
            piece = wide[pl.ds(p * 16 + q, 64, stride=32), :]
            b_l[q * 64 : q * 64 + 64, p * 128 : p * 128 + 128] = piece.astype(BF16)
    for q in range(8):
        b_lt[:, q * 128 : q * 128 + 128] = turned(b_l[q * 128 : q * 128 + 128, :])


def prepare_a(a_parts, a_bd, at):
    chunk = a_parts.astype(F32).reshape(128, 128)
    other = pltpu.roll(chunk, 64, 1)
    low = lax.broadcasted_iota(jnp.int32, (128, 128), 1) < 64
    zero = jnp.zeros((128, 128), F32)
    a_bd[0:128, pl.ds(at, 128)] = jnp.where(low, chunk, zero).astype(BF16)
    a_bd[128:256, pl.ds(at, 128)] = jnp.where(low, zero, other).astype(BF16)
    a_bd[0:128, pl.ds(at + 128, 128)] = jnp.where(low, other, zero).astype(BF16)
    a_bd[128:256, pl.ds(at + 128, 128)] = jnp.where(low, zero, chunk).astype(BF16)


def fold(y, n):
    out = []
    low = lax.broadcasted_iota(jnp.int32, (128, 128), 1) < 64
    for m in range(0, n, 2):
        e0 = y[0:128, m * 128 : m * 128 + 128]
        e1 = y[128:256, m * 128 : m * 128 + 128]
        o0 = y[0:128, m * 128 + 128 : m * 128 + 256]
        o1 = y[128:256, m * 128 + 128 : m * 128 + 256]
        out.append(jnp.where(low, e0, o1) + pltpu.roll(jnp.where(low, o0, e1), 64, 1))
    return out


MESH = pl.DeviceIdType.MESH
NB = 8
BLOCKS = 32 // NB
PEERS = 16


def dot_last(x, y):
    return lax.dot_general(x, y, (((1,), (1,)), ((), ())), preferred_element_type=F32)


def pair_block(ib, pair, cot, bias, gain, shift, wi, wit, wo, wot, b_l, a_bd, w_bd, w_bdt, xs, ps, new_pair, pair_grad):
    nb = NB
    rows = nb * 128
    at = pl.multiple_of(ib * rows, rows)
    x = dot(b_l[...], a_bd[:, pl.ds(at, rows)]).astype(BF16)
    for q in range(16):
        for k in range(nb):
            xs[k * 64 : k * 64 + 64, q * 128 : q * 128 + 128] = x[q * 64 : q * 64 + 64, k * 128 : k * 128 + 128]
    proj = dot(xs[...], w_bd[...])
    proj = jnp.concatenate(
        [proj[(k // 2) * 64 : (k // 2) * 64 + 64, (k % 2) * 128 : (k % 2) * 128 + 128] for k in range(2 * nb)], axis=0)
    updated = pair[pl.ds(at, rows), :].astype(F32) + (proj + bias[...])
    mu = jnp.mean(updated, axis=-1, keepdims=True)
    centered = updated - mu
    var = jnp.mean(centered * centered, axis=-1, keepdims=True)
    inv = lax.rsqrt(var + 1e-05)
    normed = centered * inv
    ln = (normed * gain[...] + shift[...]).astype(BF16)
    cot_here = cot[pl.ds(at, rows), :]
    both = dot(ln, wi[...])
    dh = dot(cot_here, wot[...])
    half = both[:, 0:512]
    up = both[:, 512:1024]
    q = 1.0 + jnp.tanh(half)
    act = half * q
    hidden = (act * up).astype(BF16)
    new_pair[pl.ds(at, rows), :] = (updated + dot(hidden, wo[...])).astype(BF16)
    d_up = (dh * act).astype(BF16)
    d_gate = (dh * up * (q + act * (2.0 - q))).astype(BF16)
    dn = (dot(d_gate, wit[0:512, :]) + dot(d_up, wit[512:1024, :])) * gain[...]
    m1 = jnp.mean(dn, axis=-1, keepdims=True)
    m2 = jnp.mean(dn * normed, axis=-1, keepdims=True)
    g = (cot_here.astype(F32) + inv * (dn - m1 - normed * m2)).astype(BF16)
    pair_grad[pl.ds(at, rows), :] = g
    g2 = jnp.concatenate(
        [jnp.concatenate([g[2 * k * 64 : 2 * k * 64 + 64], g[2 * k * 64 + 64 : 2 * k * 64 + 128]], axis=1) for k in range(nb)],
        axis=0)
    pulled = dot(g2, w_bdt[...]).astype(BF16)
    for q in range(16):
        for k in range(nb):
            ps[q * 64 : q * 64 + 64, pl.ds(at + k * 128, 128)] = pulled[k * 64 : k * 64 + 64, q * 128 : q * 128 + 128]


def arrived(ref, sem):
    pltpu.make_async_copy(ref, ref, sem).wait()


def kernel(
    a, b, pair_h, cot_h, weight_h, bias, gain, shift, in_h, out_h,
    new_h, pair_grad_h, grad_a, grad_b,
    pair, cot, weight, trans_in, trans_out, new_pair, pair_grad,
    a_parts, b_parts, wide, w_bd, w_bdt, wi, wit, wot, b_l, b_lt, a_bd, xs, ps,
    ga_out, ga_in, ga_sum, ga_back, gb_out, gb_in,
    load_sem, store_sem, a_send, a_recv, a_first, b_send, b_recv,
    g1_send, g1_recv, g2_send, g2_recv, gb_send, gb_recv,
):
    r, c = lax.axis_index("row"), lax.axis_index("col")
    diagonal = r == c
    off = jnp.logical_not(diagonal)
    remote = functools.partial(pltpu.make_async_remote_copy, device_id_type=MESH)

    loads = [
        pltpu.make_async_copy(x, y, load_sem.at[k])
        for k, (x, y) in enumerate(
            [(weight_h, weight), (in_h, trans_in), (out_h, trans_out), (pair_h, pair), (cot_h, cot)])
    ]
    for copy in loads:
        copy.start()

    barrier = pltpu.get_barrier_semaphore()

    def greet(where):
        pl.semaphore_signal(barrier, inc=1, device_id=where, device_id_type=MESH)

    for k in range(1, PEERS):
        greet(((r + k) % PEERS, c))
        greet((((c + k) % PEERS), r))
        greet((r, (c + k) % PEERS))

    @pl.when(off)
    def _():
        greet((c, r))

    for copy in loads[:3]:
        copy.wait()
    prepare_weights(weight, trans_in, trans_out, wide, w_bd, w_bdt, wi, wit, wot)
    pl.semaphore_wait(barrier, 3 * (PEERS - 1) + off.astype(jnp.int32))

    def b_copy(k):
        return remote(
            src_ref=b, dst_ref=b_parts.at[r], send_sem=b_send, recv_sem=b_recv, device_id=((r + k) % PEERS, c))

    def a_copy(k, ib):
        sem = a_first.at[ib] if k == 0 else a_send.at[ib]
        return remote(
            src_ref=a.at[:, pl.ds(pl.multiple_of(ib * (NB * 64), NB * 64), NB * 64)], dst_ref=a_parts.at[ib, r],
            send_sem=sem, recv_sem=a_recv.at[ib], device_id=(c, (r + k) % PEERS))

    pltpu.make_async_copy(b, b_parts.at[r], b_recv).start()
    for k in range(1, PEERS):
        b_copy(k).start()

    def give_a(ib, _):
        @pl.when(diagonal)
        def _():
            pltpu.make_async_copy(
                a.at[:, pl.ds(pl.multiple_of(ib * (NB * 64), NB * 64), NB * 64)], a_parts.at[ib, r], a_recv.at[ib]).start()

        @pl.when(off)
        def _():
            a_copy(0, ib).start()

        for k in range(1, PEERS):
            a_copy(k, ib).start()
        return 0

    lax.fori_loop(0, BLOCKS, give_a, 0)

    for copy in loads[3:]:
        copy.wait()
    arrived(b_parts, b_recv)
    prepare_b(b_parts, wide, b_l, b_lt)

    def g1_copy(k, ib):
        to = (c + k) % PEERS
        return remote(
            src_ref=ga_out.at[ib, to], dst_ref=ga_in.at[ib, c], send_sem=g1_send.at[ib], recv_sem=g1_recv.at[ib],
            device_id=(r, to))

    def g2_copy(ib):
        return remote(
            src_ref=ga_sum.at[ib], dst_ref=ga_back.at[ib], send_sem=g2_send.at[ib], recv_sem=g2_recv.at[ib], device_id=(c, r))

    def combine(ib):
        arrived(ga_in.at[ib], g1_recv.at[ib])
        for m in range(NB // 4):
            ga_sum[ib, :, m * 128 : m * 128 + 128] = jnp.sum(ga_in[ib, :, :, m * 128 : m * 128 + 128].astype(F32), axis=0)

        @pl.when(diagonal)
        def _():
            pltpu.make_async_copy(ga_sum.at[ib], ga_back.at[ib], g2_recv.at[ib]).start()

        @pl.when(off)
        def _():
            g2_copy(ib).start()

    def store(x, y, ib, k):
        part = pl.ds(pl.multiple_of(ib * (NB * 128), NB * 128), NB * 128)
        return pltpu.make_async_copy(x.at[part], y.at[part], store_sem.at[k, ib])

    def step(ib, _):
        arrived(a_parts.at[ib], a_recv.at[ib])
        at = pl.multiple_of(ib * (NB * 128), NB * 128)
        for k in range(NB // 2):
            prepare_a(a_parts[ib, :, :, k * 128 : k * 128 + 128], a_bd, at + k * 256)
        pair_block(ib, pair, cot, bias, gain, shift, wi, wit, trans_out, wot, b_l, a_bd, w_bd, w_bdt, xs, ps, new_pair, pair_grad)
        store(new_pair, new_h, ib, 0).start()
        store(pair_grad, pair_grad_h, ib, 1).start()
        pieces = fold(dot(b_lt[...], ps[:, pl.ds(at, NB * 128)]), NB)
        for m in range(NB // 4):
            two = [pieces[m + k * (NB // 4)].reshape(PEERS, 8, 128) for k in range(2)]
            ga_out[ib, :, :, m * 128 : m * 128 + 128] = jnp.concatenate(two, axis=1).astype(BF16)
        pltpu.make_async_copy(ga_out.at[ib, c], ga_in.at[ib, c], g1_recv.at[ib]).start()
        for k in range(1, PEERS):
            g1_copy(k, ib).start()

        @pl.when(ib >= 2)
        def _():
            combine(ib - 2)

        return 0

    lax.fori_loop(0, BLOCKS, step, 0)

    def gb_copy(k, h):
        to = (r + k) % PEERS
        return remote(
            src_ref=gb_out.at[h, to], dst_ref=gb_in.at[h, r], send_sem=gb_send.at[h], recv_sem=gb_recv.at[h],
            device_id=(to, c))

    for h in range(2):
        g = dot_last(a_bd[...], ps[h * 512 : h * 512 + 512, :])
        two = [g[p * 128 : p * 128 + 128].reshape(PEERS, 8, 512) for p in range(2)]
        gb_out[h] = jnp.concatenate(two, axis=1).astype(BF16)
        pltpu.make_async_copy(gb_out.at[h, r], gb_in.at[h, r], gb_recv.at[h]).start()
        for k in range(1, PEERS):
            gb_copy(k, h).start()
    combine(BLOCKS - 2)
    combine(BLOCKS - 1)

    for h in range(2):
        arrived(gb_in.at[h], gb_recv.at[h])
        for t in range(4):
            total = jnp.sum(gb_in[h, :, :, t * 128 : t * 128 + 128].astype(F32), axis=0)
            across = jnp.concatenate([total, jnp.zeros((112, 128), F32)], axis=0).T
            for k in range(2):
                q = 8 * h + 2 * t + k
                rows = across[k * 64 : k * 64 + 64]
                wide[pl.ds(q, 64, stride=32), :] = rows
                wide[pl.ds(16 + q, 64, stride=32), :] = pltpu.roll(rows, 120, 1)
    for t in range(16):
        grad_b[:, t * 128 : t * 128 + 128] = wide[t * 128 : t * 128 + 128, :].T[0:8]

    for ib in range(BLOCKS):
        arrived(ga_back.at[ib], g2_recv.at[ib])
        for k in range(2):
            at = ib * (NB * 64) + k * (NB * 32)
            grad_a[:, at : at + NB * 32] = ga_back[ib, k * 8 : k * 8 + 8, :]

    arrived(b_parts.at[0 : PEERS - 1], b_send)
    for h in range(2):
        arrived(gb_out.at[h, 0 : PEERS - 1], gb_send.at[h])
    for ib in range(BLOCKS):
        arrived(a_parts.at[ib, 0 : PEERS - 1], a_send.at[ib])
        arrived(ga_out.at[ib, 0 : PEERS - 1], g1_send.at[ib])
        store(new_pair, new_h, ib, 0).wait()
        store(pair_grad, pair_grad_h, ib, 1).wait()

        @pl.when(off)
        def _(ib=ib):
            a_copy(0, ib).wait_send()
            g2_copy(ib).wait_send()


def body(factor_a, factor_b, pair, proj_weight, proj_bias, norm_gain, norm_bias, trans_in, trans_out, cotangent):
    S = jax.ShapeDtypeStruct
    vmem = pl.BlockSpec(memory_space=pltpu.VMEM)
    hbm = pl.BlockSpec(memory_space=pl.ANY)
    V = pltpu.VMEM
    D = pltpu.SemaphoreType.DMA
    new_pair, pair_grad, grad_a, grad_b = pl.pallas_call(
        kernel,
        out_shape=(S((4096, 128), BF16), S((4096, 128), BF16), S((8, 2048), F32), S((8, 2048), F32)),
        in_specs=[vmem, vmem, hbm, hbm, hbm, vmem, vmem, vmem, hbm, hbm],
        out_specs=(hbm, hbm, vmem, vmem),
        scratch_shapes=[
            V((4096, 128), BF16), V((4096, 128), BF16), V((1024, 128), BF16), V((128, 1024), BF16), V((512, 128), BF16),
            V((4096, 128), BF16), V((4096, 128), BF16),
            V((BLOCKS, PEERS, 8, NB * 64), BF16), V((PEERS, 8, 2048), BF16),
            V((2048, 128), F32), V((2048, 256), BF16), V((256, 2048), BF16),
            V((128, 1024), BF16), V((1024, 128), BF16), V((128, 512), BF16),
            V((1024, 256), BF16), V((256, 1024), BF16), V((256, 4096), BF16),
            V((NB * 64, 2048), BF16), V((1024, 4096), BF16),
            V((BLOCKS, PEERS, 16, NB * 32), BF16), V((BLOCKS, PEERS, 16, NB * 32), BF16),
            V((BLOCKS, 16, NB * 32), F32), V((BLOCKS, 16, NB * 32), F32),
            V((2, PEERS, 16, 512), BF16), V((2, PEERS, 16, 512), BF16),
            D((5,)), D((2, BLOCKS)), D((BLOCKS,)), D((BLOCKS,)), D((BLOCKS,)), D, D,
            D((BLOCKS,)), D((BLOCKS,)), D((BLOCKS,)), D((BLOCKS,)), D((2,)), D((2,)),
        ],
        compiler_params=pltpu.CompilerParams(collective_id=0, has_side_effects=True, vmem_limit_bytes=58 << 20),
        name="whole",
    )(
        factor_a, factor_b, pair.reshape(4096, 128), cotangent.reshape(4096, 128), proj_weight,
        proj_bias.reshape(1, 128), norm_gain.reshape(1, 128), norm_bias.reshape(1, 128), trans_in, trans_out)
    return new_pair.reshape(pair.shape), pair_grad.reshape(pair.shape), grad_a, grad_b


def solution(mesh):
    tiles = P("row", "col", None)
    return jax.shard_map(
        body,
        mesh=mesh,
        in_specs=(P("row", "col"), P("row", "col"), tiles, P(), P(), P(), P(), P(), P(), tiles),
        out_specs=(tiles, tiles, P("row", "col"), P("row", "col")),
        check_vma=False,
    )
```

time: 125 us -> 72.3 us (0.58)
  Pallas kernels: 122 us -> 66.6 us
  local copies, waits for them, and re-layouts: 2.14 us -> 4.82 us
    pallas_call x3 -> x1, Pallas kernels: 122 us -> 66.6 us  [body(): pl.pallas_call(kernel, out_shape=(S((4096, 128), BF16), S((4096, 128), BF...]
    unnamed x4 -> x10, local copies, waits for them, and re-layouts: 2.14 us -> 4.82 us
where the time goes in v2:
time: 72.3 us; the launch traced here: 72 us
  Pallas kernels  66.6 us (92%)
  local copies, waits for them, and re-layouts  4.82 us (7%)
    pallas_call x1, Pallas kernels, body(): pl.pallas_call(kernel, out_shape=(S((4096, 128), BF16), S((4096, 128), BF...  66.6 us
    unnamed x10, local copies, waits for them, and re-layouts  4.82 us

profile of v2, /device:TPU:65, one launch (start us, length us, event | category | flops | bytes accessed | tf_op | source)
XLA Modules:
  0.0 72.0 jit_solution(4997774020987791728)
XLA Ops:
  0.6 66.6 %whole.1 = (bf16[4096,128]{1,0:T(8,128)(2,1)}, bf16[4096,128]{1,0:T(8,128)(2,1)}, f32[8,2048]{1,0:T(8,128)}, f32[8,2048]{1,0:T(8,128)}) custom-call(bf16[8,2048]{1,0:T(8,128)(2,1)} %a.1, bf16[8,2048]{1,0:T(8,128)(2,1)} %b.1, bf16[4096,128]{1,0:T(8,128)(2,1)} %bitcast.7, bf16[4096,128]{1,0:T(8,128)(2,1)} %bitcast.8, bf16[1024,128]{1,0:T(8,128)(2,1)} %weight_h.1, ...), custom_call_target="tpu_custom_call" | custom-call | tf_op jit(solution)/shard_map/whole/pallas_call | solution.py:313
  67.2 0.0 copy-start
  67.2 2.4 %copy.18 = bf16[64,64,128]{2,1,0:T(8,128)(2,1)} copy(bf16[64,64,128]{2,1,0:T(8,128)(2,1)} %bitcast.10) | data formatting | bytes 2097152
  69.6 0.0 copy-done
  69.6 0.0 copy-start.2
  69.6 1.0 %copy.19 = bf16[64,64,128]{2,1,0:T(8,128)(2,1)} copy(bf16[64,64,128]{2,1,0:T(8,128)(2,1)S(1)} %bitcast.9) | data formatting | bytes 2097152
  70.5 0.0 copy-done.2
  70.5 0.0 copy-start.1
  70.6 0.6 copy.20
  71.2 0.2 copy-done.1
  71.4 0.6 copy.21
Async XLA Ops:
  67.2 2.4 %copy-start = (bf16[4096,128]{1,0:T(8,128)(2,1)S(1)}, bf16[4096,128]{1,0:T(8,128)(2,1)}, u32[]{:S(2)}) copy-start(bf16[4096,128]{1,0:T(8,128)(2,1)} %get-tuple-element.9) | copy-start | bytes 3145732
  69.6 1.0 %copy-start.2 = (f32[8,2048]{1,0:T(8,128)S(1)}, f32[8,2048]{1,0:T(8,128)}, u32[]{:S(2)}) copy-start(f32[8,2048]{1,0:T(8,128)} %get-tuple-element.18) | copy-start | bytes 196612
  70.5 0.9 %copy-start.1 = (f32[8,2048]{1,0:T(8,128)S(1)}, f32[8,2048]{1,0:T(8,128)}, u32[]{:S(2)}) copy-start(f32[8,2048]{1,0:T(8,128)} %get-tuple-element.19) | copy-start | bytes 196612

commit v3 on v2

--- a/solution.py
+++ b/solution.py
@@ -73,6 +73,8 @@
 MESH = pl.DeviceIdType.MESH
 NB = 8
 BLOCKS = 32 // NB
+ROWS = NB * 128
+CHUNK = 256
 PEERS = 16
 
 
@@ -80,46 +82,66 @@
     return lax.dot_general(x, y, (((1,), (1,)), ((), ())), preferred_element_type=F32)
 
 
-def pair_block(ib, pair, cot, bias, gain, shift, wi, wit, wo, wot, b_l, a_bd, w_bd, w_bdt, xs, ps, new_pair, pair_grad):
-    nb = NB
-    rows = nb * 128
-    at = pl.multiple_of(ib * rows, rows)
-    x = dot(b_l[...], a_bd[:, pl.ds(at, rows)]).astype(BF16)
-    for q in range(16):
-        for k in range(nb):
-            xs[k * 64 : k * 64 + 64, q * 128 : q * 128 + 128] = x[q * 64 : q * 64 + 64, k * 128 : k * 128 + 128]
-    proj = dot(xs[...], w_bd[...])
-    proj = jnp.concatenate(
-        [proj[(k // 2) * 64 : (k // 2) * 64 + 64, (k % 2) * 128 : (k % 2) * 128 + 128] for k in range(2 * nb)], axis=0)
-    updated = pair[pl.ds(at, rows), :].astype(F32) + (proj + bias[...])
+def projected(ib, b_l, a_bd, w_bd, proj):
+    at = pl.multiple_of(ib * ROWS, ROWS)
+    for c in range(4):
+        x = dot(b_l[c * 256 : c * 256 + 256, :], a_bd[:, pl.ds(at, ROWS)]).astype(BF16)
+        x = jnp.concatenate(
+            [
+                jnp.concatenate([x[q * 64 : q * 64 + 64, k * 128 : k * 128 + 128] for q in range(4)], axis=1)
+                for k in range(NB)
+            ],
+            axis=0)
+        part = dot(x, w_bd[c * 512 : c * 512 + 512, :])
+        if c == 0:
+            proj[...] = part
+        else:
+            proj[...] += part
+
+
+def pair_rows(at, first, pair, cot, proj, bias, gain, shift, wi, wit, wot, updated_all, hidden_all, pair_grad):
+    here = pl.ds(at, CHUNK)
+    parts = [
+        proj[(k // 2) * 64 : (k // 2) * 64 + 64, (k % 2) * 128 : (k % 2) * 128 + 128]
+        for k in range(first // 64, (first + CHUNK) // 64)
+    ]
+    updated = pair[here, :].astype(F32) + (jnp.concatenate(parts, axis=0) + bias[...])
+    updated_all[here, :] = updated
     mu = jnp.mean(updated, axis=-1, keepdims=True)
     centered = updated - mu
     var = jnp.mean(centered * centered, axis=-1, keepdims=True)
     inv = lax.rsqrt(var + 1e-05)
     normed = centered * inv
     ln = (normed * gain[...] + shift[...]).astype(BF16)
-    cot_here = cot[pl.ds(at, rows), :]
-    both = dot(ln, wi[...])
+    cot_here = cot[here, :]
+    half = dot(ln, wi[:, 0:512])
+    up = dot(ln, wi[:, 512:1024])
     dh = dot(cot_here, wot[...])
-    half = both[:, 0:512]
-    up = both[:, 512:1024]
     q = 1.0 + jnp.tanh(half)
     act = half * q
-    hidden = (act * up).astype(BF16)
-    new_pair[pl.ds(at, rows), :] = (updated + dot(hidden, wo[...])).astype(BF16)
+    hidden_all[here, :] = (act * up).astype(BF16)
     d_up = (dh * act).astype(BF16)
     d_gate = (dh * up * (q + act * (2.0 - q))).astype(BF16)
-    dn = (dot(d_gate, wit[0:512, :]) + dot(d_up, wit[512:1024, :])) * gain[...]
+    dn = dot(jnp.concatenate([d_gate, d_up], axis=1), wit[...]) * gain[...]
     m1 = jnp.mean(dn, axis=-1, keepdims=True)
     m2 = jnp.mean(dn * normed, axis=-1, keepdims=True)
     g = (cot_here.astype(F32) + inv * (dn - m1 - normed * m2)).astype(BF16)
-    pair_grad[pl.ds(at, rows), :] = g
-    g2 = jnp.concatenate(
-        [jnp.concatenate([g[2 * k * 64 : 2 * k * 64 + 64], g[2 * k * 64 + 64 : 2 * k * 64 + 128]], axis=1) for k in range(nb)],
-        axis=0)
-    pulled = dot(g2, w_bdt[...]).astype(BF16)
+    pair_grad[here, :] = g
+    return [
+        jnp.concatenate([g[k * 128 : k * 128 + 64], g[k * 128 + 64 : k * 128 + 128]], axis=1) for k in range(CHUNK // 128)
+    ]
+
+
+def pair_block(ib, pair, cot, bias, gain, shift, wi, wit, wot, b_l, a_bd, w_bd, w_bdt, proj, ps, updated_all, hidden_all, pair_grad):
+    at = pl.multiple_of(ib * ROWS, ROWS)
+    projected(ib, b_l, a_bd, w_bd, proj)
+    sides = []
+    for first in range(0, ROWS, CHUNK):
+        sides += pair_rows(
+            at + first, first, pair, cot, proj, bias, gain, shift, wi, wit, wot, updated_all, hidden_all, pair_grad)
+    pulled = dot(jnp.concatenate(sides, axis=0), w_bdt[...]).astype(BF16)
     for q in range(16):
-        for k in range(nb):
+        for k in range(NB):
             ps[q * 64 : q * 64 + 64, pl.ds(at + k * 128, 128)] = pulled[k * 64 : k * 64 + 64, q * 128 : q * 128 + 128]
 
 
@@ -129,9 +151,9 @@
 
 def kernel(
     a, b, pair_h, cot_h, weight_h, bias, gain, shift, in_h, out_h,
-    new_h, pair_grad_h, grad_a, grad_b,
+    new_h, pair_grad_h, grad_a, gb_sum,
     pair, cot, weight, trans_in, trans_out, new_pair, pair_grad,
-    a_parts, b_parts, wide, w_bd, w_bdt, wi, wit, wot, b_l, b_lt, a_bd, xs, ps,
+    a_parts, b_parts, wide, w_bd, w_bdt, wi, wit, wot, b_l, b_lt, a_bd, proj, ps, updated_all, hidden_all,
     ga_out, ga_in, ga_sum, ga_back, gb_out, gb_in,
     load_sem, store_sem, a_send, a_recv, a_first, b_send, b_recv,
     g1_send, g1_recv, g2_send, g2_recv, gb_send, gb_recv,
@@ -163,9 +185,6 @@
     def _():
         greet((c, r))
 
-    for copy in loads[:3]:
-        copy.wait()
-    prepare_weights(weight, trans_in, trans_out, wide, w_bd, w_bdt, wi, wit, wot)
     pl.semaphore_wait(barrier, 3 * (PEERS - 1) + off.astype(jnp.int32))
 
     def b_copy(k):
@@ -198,8 +217,9 @@
 
     lax.fori_loop(0, BLOCKS, give_a, 0)
 
-    for copy in loads[3:]:
+    for copy in loads:
         copy.wait()
+    prepare_weights(weight, trans_in, trans_out, wide, w_bd, w_bdt, wi, wit, wot)
     arrived(b_parts, b_recv)
     prepare_b(b_parts, wide, b_l, b_lt)
 
@@ -235,13 +255,13 @@
         at = pl.multiple_of(ib * (NB * 128), NB * 128)
         for k in range(NB // 2):
             prepare_a(a_parts[ib, :, :, k * 128 : k * 128 + 128], a_bd, at + k * 256)
-        pair_block(ib, pair, cot, bias, gain, shift, wi, wit, trans_out, wot, b_l, a_bd, w_bd, w_bdt, xs, ps, new_pair, pair_grad)
-        store(new_pair, new_h, ib, 0).start()
+        pair_block(
+            ib, pair, cot, bias, gain, shift, wi, wit, wot, b_l, a_bd, w_bd, w_bdt, proj, ps, updated_all, hidden_all, pair_grad)
         store(pair_grad, pair_grad_h, ib, 1).start()
-        pieces = fold(dot(b_lt[...], ps[:, pl.ds(at, NB * 128)]), NB)
-        for m in range(NB // 4):
-            two = [pieces[m + k * (NB // 4)].reshape(PEERS, 8, 128) for k in range(2)]
-            ga_out[ib, :, :, m * 128 : m * 128 + 128] = jnp.concatenate(two, axis=1).astype(BF16)
+        for k in range(2):
+            pieces = fold(dot(b_lt[...], ps[:, pl.ds(at + k * (NB * 64), NB * 64)]), NB // 2)
+            for m, piece in enumerate(pieces):
+                ga_out[ib, :, k * 8 : k * 8 + 8, m * 128 : m * 128 + 128] = piece.reshape(PEERS, 8, 128).astype(BF16)
         pltpu.make_async_copy(ga_out.at[ib, c], ga_in.at[ib, c], g1_recv.at[ib]).start()
         for k in range(1, PEERS):
             g1_copy(k, ib).start()
@@ -268,20 +288,21 @@
         for k in range(1, PEERS):
             gb_copy(k, h).start()
     combine(BLOCKS - 2)
+
+    def finish_new(ib, _):
+        here = pl.ds(pl.multiple_of(ib * ROWS, ROWS), ROWS)
+        new_pair[here, :] = (updated_all[here, :] + dot(hidden_all[here, :], trans_out[...])).astype(BF16)
+        store(new_pair, new_h, ib, 0).start()
+        return 0
+
+    lax.fori_loop(0, BLOCKS, finish_new, 0)
     combine(BLOCKS - 1)
 
     for h in range(2):
         arrived(gb_in.at[h], gb_recv.at[h])
         for t in range(4):
-            total = jnp.sum(gb_in[h, :, :, t * 128 : t * 128 + 128].astype(F32), axis=0)
-            across = jnp.concatenate([total, jnp.zeros((112, 128), F32)], axis=0).T
-            for k in range(2):
-                q = 8 * h + 2 * t + k
-                rows = across[k * 64 : k * 64 + 64]
-                wide[pl.ds(q, 64, stride=32), :] = rows
-                wide[pl.ds(16 + q, 64, stride=32), :] = pltpu.roll(rows, 120, 1)
-    for t in range(16):
-        grad_b[:, t * 128 : t * 128 + 128] = wide[t * 128 : t * 128 + 128, :].T[0:8]
+            gb_sum[:, h * 512 + t * 128 : h * 512 + t * 128 + 128] = jnp.sum(
+                gb_in[h, :, :, t * 128 : t * 128 + 128].astype(F32), axis=0)
 
     for ib in range(BLOCKS):
         arrived(ga_back.at[ib], g2_recv.at[ib])
@@ -304,15 +325,41 @@
             g2_copy(ib).wait_send()
 
 
+def finish_kernel(new_h, pair_grad_h, grad_a_h, gb_sum, new_o, pair_grad_o, grad_a_o, grad_b, new, pair_grad, grad_a, wide, in_sem, out_sem):
+    pieces = []
+    for k in range(4):
+        part = slice(k * 1024, k * 1024 + 1024)
+        pieces += [(new_h, new, new_o, part), (pair_grad_h, pair_grad, pair_grad_o, part)]
+    pieces.append((grad_a_h, grad_a, grad_a_o, slice(0, 8)))
+    ins = [pltpu.make_async_copy(x.at[p], y.at[p], in_sem.at[k]) for k, (x, y, _, p) in enumerate(pieces)]
+    outs = [pltpu.make_async_copy(y.at[p], z.at[p], out_sem.at[k]) for k, (_, y, z, p) in enumerate(pieces)]
+    for copy in ins:
+        copy.start()
+    for before, after in zip(ins, outs):
+        before.wait()
+        after.start()
+    for t in range(8):
+        across = jnp.concatenate([gb_sum[:, t * 128 : t * 128 + 128], jnp.zeros((112, 128), F32)], axis=0).T
+        for k in range(2):
+            q = 2 * t + k
+            rows = across[k * 64 : k * 64 + 64]
+            wide[pl.ds(q, 64, stride=32), :] = rows
+            wide[pl.ds(16 + q, 64, stride=32), :] = pltpu.roll(rows, 120, 1)
+    for t in range(16):
+        grad_b[:, t * 128 : t * 128 + 128] = wide[t * 128 : t * 128 + 128, :].T[0:8]
+    for copy in outs:
+        copy.wait()
+
+
 def body(factor_a, factor_b, pair, proj_weight, proj_bias, norm_gain, norm_bias, trans_in, trans_out, cotangent):
     S = jax.ShapeDtypeStruct
     vmem = pl.BlockSpec(memory_space=pltpu.VMEM)
     hbm = pl.BlockSpec(memory_space=pl.ANY)
     V = pltpu.VMEM
     D = pltpu.SemaphoreType.DMA
-    new_pair, pair_grad, grad_a, grad_b = pl.pallas_call(
+    new_pair, pair_grad, grad_a, gb_sum = pl.pallas_call(
         kernel,
-        out_shape=(S((4096, 128), BF16), S((4096, 128), BF16), S((8, 2048), F32), S((8, 2048), F32)),
+        out_shape=(S((4096, 128), BF16), S((4096, 128), BF16), S((8, 2048), F32), S((16, 1024), F32)),
         in_specs=[vmem, vmem, hbm, hbm, hbm, vmem, vmem, vmem, hbm, hbm],
         out_specs=(hbm, hbm, vmem, vmem),
         scratch_shapes=[
@@ -322,7 +369,7 @@
             V((2048, 128), F32), V((2048, 256), BF16), V((256, 2048), BF16),
             V((128, 1024), BF16), V((1024, 128), BF16), V((128, 512), BF16),
             V((1024, 256), BF16), V((256, 1024), BF16), V((256, 4096), BF16),
-            V((NB * 64, 2048), BF16), V((1024, 4096), BF16),
+            V((NB * 64, 256), F32), V((1024, 4096), BF16), V((4096, 128), F32), V((4096, 512), BF16),
             V((BLOCKS, PEERS, 16, NB * 32), BF16), V((BLOCKS, PEERS, 16, NB * 32), BF16),
             V((BLOCKS, 16, NB * 32), F32), V((BLOCKS, 16, NB * 32), F32),
             V((2, PEERS, 16, 512), BF16), V((2, PEERS, 16, 512), BF16),
@@ -334,6 +381,14 @@
     )(
         factor_a, factor_b, pair.reshape(4096, 128), cotangent.reshape(4096, 128), proj_weight,
         proj_bias.reshape(1, 128), norm_gain.reshape(1, 128), norm_bias.reshape(1, 128), trans_in, trans_out)
+    new_pair, pair_grad, grad_a, grad_b = pl.pallas_call(
+        finish_kernel,
+        out_shape=(S((4096, 128), BF16), S((4096, 128), BF16), S((8, 2048), F32), S((8, 2048), F32)),
+        in_specs=[hbm, hbm, hbm, vmem],
+        out_specs=(hbm, hbm, hbm, vmem),
+        scratch_shapes=[V((4096, 128), BF16), V((4096, 128), BF16), V((8, 2048), F32), V((2048, 128), F32), D((9,)), D((9,))],
+        name="finish",
+    )(new_pair, pair_grad, grad_a, gb_sum)
     return new_pair.reshape(pair.shape), pair_grad.reshape(pair.shape), grad_a, grad_b
 
 

time: 72.3 us -> 66.9 us (0.925)
  local copies, waits for them, and re-layouts: 4.82 us -> 0 us
  Pallas kernels: 66.6 us -> 65.8 us
    pallas_call x1, Pallas kernels: 66.6 us -> 61.6 us  [body(): pl.pallas_call(kernel, out_shape=(S((4096, 128), BF16), S((4096, 128), BF...]
    unnamed x10 -> x0, local copies, waits for them, and re-layouts: 4.82 us -> none
    pallas_call x0 -> x1, Pallas kernels: none -> 4.24 us  [body(): pl.pallas_call(finish_kernel, out_shape=(S((4096, 128), BF16), S((4096, 1...]
where the time goes in v3:
time: 66.9 us; the launch traced here: 66.5 us
  Pallas kernels  65.8 us (98%)
    pallas_call x1, Pallas kernels, body(): pl.pallas_call(kernel, out_shape=(S((4096, 128), BF16), S((4096, 128), BF...  61.6 us
    pallas_call x1, Pallas kernels, body(): pl.pallas_call(finish_kernel, out_shape=(S((4096, 128), BF16), S((4096, 1...  4.24 us

profile of v3, /device:TPU:65, one launch (start us, length us, event | category | flops | bytes accessed | tf_op | source)
XLA Modules:
  0.0 66.5 jit_solution(6766013192014226199)
XLA Ops:
  0.6 61.6 %whole.1 = (bf16[4096,128]{1,0:T(8,128)(2,1)}, bf16[4096,128]{1,0:T(8,128)(2,1)}, f32[8,2048]{1,0:T(8,128)}, f32[16,1024]{1,0:T(8,128)}) custom-call(bf16[8,2048]{1,0:T(8,128)(2,1)} %a.1, bf16[8,2048]{1,0:T(8,128)(2,1)} %b.1, bf16[4096,128]{1,0:T(8,128)(2,1)} %bitcast.7, bf16[4096,128]{1,0:T(8,128)(2,1)} %bitcast.8, bf16[1024,128]{1,0:T(8,128)(2,1)} %weight_h.1, ...), custom_call_target="tpu_custom_call" | custom-call | tf_op jit(solution)/shard_map/whole/pallas_call | solution.py:360
  62.2 4.2 %finish.1 = (bf16[4096,128]{1,0:T(8,128)(2,1)}, bf16[4096,128]{1,0:T(8,128)(2,1)}, f32[8,2048]{1,0:T(8,128)}, f32[8,2048]{1,0:T(8,128)}) custom-call(bf16[4096,128]{1,0:T(8,128)(2,1)} %get-tuple-element.12.new_h, bf16[4096,128]{1,0:T(8,128)(2,1)} %get-tuple-element.13.pair_grad_h, f32[8,2048]{1,0:T(8,128)} %get-tuple-element.14.grad_a_h, ...), custom_call_target="tpu_custom_call" | custom-call | tf_op jit(solution)/shard_map/finish/pallas_call | solution.py:384

commit v4 on v3

--- a/solution.py
+++ b/solution.py
@@ -197,10 +197,6 @@
             src_ref=a.at[:, pl.ds(pl.multiple_of(ib * (NB * 64), NB * 64), NB * 64)], dst_ref=a_parts.at[ib, r],
             send_sem=sem, recv_sem=a_recv.at[ib], device_id=(c, (r + k) % PEERS))
 
-    pltpu.make_async_copy(b, b_parts.at[r], b_recv).start()
-    for k in range(1, PEERS):
-        b_copy(k).start()
-
     def give_a(ib, _):
         @pl.when(diagonal)
         def _():
@@ -215,7 +211,11 @@
             a_copy(k, ib).start()
         return 0
 
-    lax.fori_loop(0, BLOCKS, give_a, 0)
+    give_a(0, 0)
+    pltpu.make_async_copy(b, b_parts.at[r], b_recv).start()
+    for k in range(1, PEERS):
+        b_copy(k).start()
+    lax.fori_loop(1, BLOCKS, give_a, 0)
 
     for copy in loads:
         copy.wait()
@@ -335,9 +335,6 @@
     outs = [pltpu.make_async_copy(y.at[p], z.at[p], out_sem.at[k]) for k, (_, y, z, p) in enumerate(pieces)]
     for copy in ins:
         copy.start()
-    for before, after in zip(ins, outs):
-        before.wait()
-        after.start()
     for t in range(8):
         across = jnp.concatenate([gb_sum[:, t * 128 : t * 128 + 128], jnp.zeros((112, 128), F32)], axis=0).T
         for k in range(2):
@@ -345,6 +342,9 @@
             rows = across[k * 64 : k * 64 + 64]
             wide[pl.ds(q, 64, stride=32), :] = rows
             wide[pl.ds(16 + q, 64, stride=32), :] = pltpu.roll(rows, 120, 1)
+    for before, after in zip(ins, outs):
+        before.wait()
+        after.start()
     for t in range(16):
         grad_b[:, t * 128 : t * 128 + 128] = wide[t * 128 : t * 128 + 128, :].T[0:8]
     for copy in outs:

time: 66.9 us -> 67.3 us (level)
  no operation moved by 1% of the time
where the time goes in v4:
time: 67.3 us; the launch traced here: 67.1 us
  Pallas kernels  66.4 us (99%)
    pallas_call x1, Pallas kernels, body(): pl.pallas_call(kernel, out_shape=(S((4096, 128), BF16), S((4096, 128), BF...  62.1 us
    pallas_call x1, Pallas kernels, body(): pl.pallas_call(finish_kernel, out_shape=(S((4096, 128), BF16), S((4096, 1...  4.28 us

profile of v4, /device:TPU:65, one launch (start us, length us, event | category | flops | bytes accessed | tf_op | source)
XLA Modules:
  0.0 67.1 jit_solution(6041350575050120302)
XLA Ops:
  0.6 62.1 %whole.1 = (bf16[4096,128]{1,0:T(8,128)(2,1)}, bf16[4096,128]{1,0:T(8,128)(2,1)}, f32[8,2048]{1,0:T(8,128)}, f32[16,1024]{1,0:T(8,128)}) custom-call(bf16[8,2048]{1,0:T(8,128)(2,1)} %a.1, bf16[8,2048]{1,0:T(8,128)(2,1)} %b.1, bf16[4096,128]{1,0:T(8,128)(2,1)} %bitcast.7, bf16[4096,128]{1,0:T(8,128)(2,1)} %bitcast.8, bf16[1024,128]{1,0:T(8,128)(2,1)} %weight_h.1, ...), custom_call_target="tpu_custom_call" | custom-call | tf_op jit(solution)/shard_map/whole/pallas_call | solution.py:360
  62.8 4.3 %finish.1 = (bf16[4096,128]{1,0:T(8,128)(2,1)}, bf16[4096,128]{1,0:T(8,128)(2,1)}, f32[8,2048]{1,0:T(8,128)}, f32[8,2048]{1,0:T(8,128)}) custom-call(bf16[4096,128]{1,0:T(8,128)(2,1)} %get-tuple-element.12.new_h, bf16[4096,128]{1,0:T(8,128)(2,1)} %get-tuple-element.13.pair_grad_h, f32[8,2048]{1,0:T(8,128)} %get-tuple-element.14.grad_a_h, ...), custom_call_target="tpu_custom_call" | custom-call | tf_op jit(solution)/shard_map/finish/pallas_call | solution.py:384

commit v5 on v3

--- a/solution.py
+++ b/solution.py
@@ -71,7 +71,7 @@
 
 
 MESH = pl.DeviceIdType.MESH
-NB = 8
+NB = 16
 BLOCKS = 32 // NB
 ROWS = NB * 128
 CHUNK = 256

time: 66.9 us -> 68.2 us (1.019)
  the two profiles are of different devices: /device:TPU:65 before, /device:TPU:5 now
where the time goes in v5:
time: 68.2 us; the launch traced here: 68 us
  Pallas kernels  67.2 us (99%)
  between operations  0.8 us (1%)
    pallas_call x1, Pallas kernels, body(): pl.pallas_call(kernel, out_shape=(S((4096, 128), BF16), S((4096, 128), BF...  62.9 us
    pallas_call x1, Pallas kernels, body(): pl.pallas_call(finish_kernel, out_shape=(S((4096, 128), BF16), S((4096, 1...  4.24 us

profile of v5, /device:TPU:5, one launch (start us, length us, event | category | flops | bytes accessed | tf_op | source)
XLA Modules:
  0.0 68.0 jit_solution(17998029095097914723)
XLA Ops:
  0.6 62.9 %whole.1 = (bf16[4096,128]{1,0:T(8,128)(2,1)}, bf16[4096,128]{1,0:T(8,128)(2,1)}, f32[8,2048]{1,0:T(8,128)}, f32[16,1024]{1,0:T(8,128)}) custom-call(bf16[8,2048]{1,0:T(8,128)(2,1)} %a.1, bf16[8,2048]{1,0:T(8,128)(2,1)} %b.1, bf16[4096,128]{1,0:T(8,128)(2,1)} %bitcast.7, bf16[4096,128]{1,0:T(8,128)(2,1)} %bitcast.8, bf16[1024,128]{1,0:T(8,128)(2,1)} %weight_h.1, ...), custom_call_target="tpu_custom_call" | custom-call | tf_op jit(solution)/shard_map/whole/pallas_call | solution.py:360
  63.6 4.2 %finish.1 = (bf16[4096,128]{1,0:T(8,128)(2,1)}, bf16[4096,128]{1,0:T(8,128)(2,1)}, f32[8,2048]{1,0:T(8,128)}, f32[8,2048]{1,0:T(8,128)}) custom-call(bf16[4096,128]{1,0:T(8,128)(2,1)} %get-tuple-element.12.new_h, bf16[4096,128]{1,0:T(8,128)(2,1)} %get-tuple-element.13.pair_grad_h, f32[8,2048]{1,0:T(8,128)} %get-tuple-element.14.grad_a_h, ...), custom_call_target="tpu_custom_call" | custom-call | tf_op jit(solution)/shard_map/finish/pallas_call | solution.py:384
